TPU v7x, 32 devices: a whole 2x2x4 slice. The times are simulated.
32 devices in a mesh: grp: 4 (over y, x), seq: 8 (over z, core).
Axes of the slice: x: 2, y: 2, z: 4, core: 2. Of those that a mesh axis runs over, the one named last changes fastest.
Arguments:
- queries: bfloat16 [1024, 64, 192], P('seq', 'grp'), may hold values from -6 to 6
- key_cache: bfloat16 [4, 8192, 192], P('grp', 'seq'), may hold values from -6 to 6
- group_value_cache: bfloat16 [4, 8192, 128], P('grp', 'seq'), may hold values from -6 to 6
- coarse_keys: bfloat16 [4, 512, 192], P('grp', 'seq'), may hold values from -6 to 6
- coarse_values: bfloat16 [4, 512, 128], P('grp', 'seq'), may hold values from -6 to 6
- hidden: bfloat16 [1024, 2560], P('seq'), may hold values from -6 to 6
- gate_weight: bfloat16 [4, 2560, 32], P('grp'), may hold values from -0.125 to 0.125
- out_weight: bfloat16 [8192, 2560], P('grp'), may hold values from -0.09375 to 0.09375
- selected: int32 [4, 8, 16], P('grp', 'seq'), may hold values from 0 to 127, as said below
Outputs:
- layer_out: bfloat16 [1024, 2560], P('seq', 'grp')
Inputs may be any that keep to these rules, and one draw needn't show every extreme that they name: selected[g, t] lists 16 distinct blocks of 64 positions for tile t of group g; the first is block 0; none starts after the tile's last query position; at most 4 of them lie within one index of seq's 1024 positions.
All inputs are finite; a program needn't handle non-finite values.
Results may differ from a plain program's by a relative error of at most 0.013.
Values may be sent and summed in bfloat16 or wider, within the bound.
A program may use at most 128 MiB of HBM per device.

v0:
```python
import math

import jax
import jax.numpy as jnp
from jax import lax
from jax.sharding import PartitionSpec as P

BLK = 64
SEL = 16
TILE = 128
CSTRIDE = 16
CLEN = 32


NEGATIVE = -1e30


def online_block(folded, part_keys, part_values, query_rows, row_pos, key_pos, score_scale):
    running, row_total, summed_out = folded
    logit_scores = (
        lax.dot_general(
            query_rows, part_keys, (((1,), (1,)), ((), ())), preferred_element_type=jnp.float32
        )
        * score_scale
    )
    logit_scores = jnp.where(key_pos[None, :] <= row_pos[:, None], logit_scores, -jnp.inf)
    new_max = jnp.maximum(running, jnp.max(logit_scores, axis=1))
    factor = jnp.exp(running - new_max)
    weights = jnp.exp(logit_scores - new_max[:, None])
    row_total = row_total * factor + jnp.sum(weights, axis=1)
    summed_out = summed_out * factor[:, None] + jnp.dot(
        weights.astype(jnp.bfloat16), part_values, preferred_element_type=jnp.float32
    )
    return (new_max, row_total, summed_out)


def shards(
    queries,
    key_cache,
    group_value_cache,
    coarse_keys,
    coarse_values,
    hidden,
    gate_weight,
    out_weight,
    selected,
):
    seq_count = lax.axis_size("seq")
    seq_index = lax.axis_index("seq")
    ctx_dev = key_cache.shape[1]
    context = ctx_dev * seq_count
    heads_here = queries.shape[1]
    key_width = queries.shape[2]
    value_width = group_value_cache.shape[2]
    score_scale = key_width ** (-0.5)
    query_rows = queries.reshape(TILE * heads_here, key_width)
    query_pos = context - TILE * seq_count + seq_index * TILE + jnp.arange(TILE, dtype=jnp.int32)
    row_pos = jnp.repeat(query_pos, heads_here)
    row_count = TILE * heads_here
    fold_start = (
        jnp.full((row_count,), NEGATIVE, jnp.float32),
        jnp.zeros((row_count,), jnp.float32),
        jnp.zeros((row_count, value_width), jnp.float32),
    )
    requests = lax.all_gather(selected[0], "seq", axis=0, tiled=True)
    blocks_dev = ctx_dev // BLK
    slot_cap = max(1, 2 * SEL // seq_count)
    owners = requests // blocks_dev
    earlier = jnp.tril(jnp.ones((SEL, SEL), jnp.int32), -1)
    same_owner = (owners[:, :, None] == owners[:, None, :]).astype(jnp.int32)
    order_rank = jnp.sum(same_owner * earlier[None], axis=2)
    served = owners == seq_index
    slot_ids = jnp.arange(slot_cap, dtype=jnp.int32)
    matches = (served[:, :, None] & (order_rank[:, :, None] == slot_ids[None, None, :])).astype(
        jnp.int32
    )
    local_block = jnp.sum(matches * (requests - seq_index * blocks_dev)[:, :, None], axis=1)
    filled = jnp.sum(matches, axis=1) > 0
    block_keys_grouped = key_cache[0].reshape(blocks_dev, BLK, key_width)
    value_blocks = group_value_cache[0].reshape(blocks_dev, BLK, value_width)
    outgoing = jnp.concatenate(
        [
            jnp.take(block_keys_grouped, local_block, axis=0),
            jnp.take(value_blocks, local_block, axis=0),
        ],
        axis=3,
    )
    outgoing = jnp.where(filled[:, :, None, None], outgoing, jnp.zeros_like(outgoing))
    incoming = lax.all_to_all(outgoing, "seq", split_axis=0, concat_axis=0, tiled=True)
    piece_keys = lax.all_gather(coarse_keys[0], "seq", axis=0, tiled=True)
    piece_values = lax.all_gather(coarse_values[0], "seq", axis=0, tiled=True)
    length = piece_keys.shape[0]
    span_rows = math.gcd(length, 512)

    def advance(loop_index, state_now):
        offset = loop_index * span_rows
        part_keys = lax.dynamic_slice_in_dim(piece_keys, offset, span_rows, 0)
        part_values = lax.dynamic_slice_in_dim(piece_values, offset, span_rows, 0)
        key_pos = (offset + jnp.arange(span_rows, dtype=jnp.int32)) * CSTRIDE + CLEN - 1
        return online_block(
            state_now, part_keys, part_values, query_rows, row_pos, key_pos, score_scale
        )

    coarse_state = lax.fori_loop(0, length // span_rows, advance, fold_start)
    coarse_out = coarse_state[2] / coarse_state[1][:, None]
    own_list = selected[0, 0]
    own_owner = own_list // blocks_dev
    own_rank = jnp.sum(
        (own_owner[:, None] == own_owner[None, :]).astype(jnp.int32) * earlier, axis=1
    )
    picked_rows = incoming[own_owner, own_rank].reshape(SEL * BLK, key_width + value_width)
    picked_keys = picked_rows[:, :key_width]
    picked_values = picked_rows[:, key_width:]
    picked_pos = (own_list[:, None] * BLK + jnp.arange(BLK, dtype=jnp.int32)[None, :]).reshape(-1)
    picked_state = online_block(
        fold_start, picked_keys, picked_values, query_rows, row_pos, picked_pos, score_scale
    )
    picked_out = picked_state[2] / picked_state[1][:, None]
    gate_logits = jnp.dot(hidden, gate_weight[0], preferred_element_type=jnp.float32)
    gate_coarse = jax.nn.sigmoid(gate_logits[:, :heads_here])
    gate_picked = jax.nn.sigmoid(gate_logits[:, heads_here:])
    mixed_heads = gate_coarse[:, :, None] * coarse_out.reshape(
        TILE, heads_here, value_width
    ) + gate_picked[:, :, None] * picked_out.reshape(TILE, heads_here, value_width)
    attended = mixed_heads.astype(jnp.bfloat16).reshape(TILE, heads_here * value_width)
    partial_value = jnp.dot(attended, out_weight, preferred_element_type=jnp.float32)
    result = lax.psum_scatter(
        partial_value.astype(jnp.bfloat16), "grp", scatter_dimension=1, tiled=True
    )
    return result


def solution(mesh):
    return jax.shard_map(
        shards,
        mesh=mesh,
        in_specs=(
            P("seq", "grp", None),
            P("grp", "seq", None),
            P("grp", "seq", None),
            P("grp", "seq", None),
            P("grp", "seq", None),
            P("seq", None),
            P("grp", None, None),
            P("grp", None),
            P("grp", "seq", None),
        ),
        out_specs=P("seq", "grp"),
        check_vma=False,
    )
```

profile of v0, /device:TPU:8, one launch (start us, length us, event | category | flops | bytes accessed | tf_op | source)
XLA Modules:
  0.0 152.7 jit_solution(9140498446499711631)
XLA Ops:
  6.5 9.3 %all-gather.2 = s32[8,1,16]{2,1,0:T(1,128)S(1)} all-gather(s32[1,1,16]{2,1,0:T(1,128)} %param.17), channel_id=4, replica_groups=mesh['grp'=4,'seq'=8] {'seq'}, dimensions={0}, use_global_device_ids=true | all-gather | bytes 576 | tf_op jit(solution)/shard_map/all_gather | solution.py:65
  15.8 0.7 bitcast_multiply_fusion.2
  17.5 1.2 copy.40
  18.7 0.6 gather_fusion
  19.4 1.6 %gather_fusion.1 = bf16[32,64,128]{2,1,0:T(8,128)(2,1)S(1)} fusion(bf16[16,64,128]{2,1,0:T(8,128)(2,1)} %bitcast.90, s32[1024]{0:T(1024)S(1)} %pad_clamp_fusion), kind=kCustom, calls=%fused_computation.1 | custom fusion | bytes 1048704 | tf_op jit(solution)/shard_map/jit(_take)/gather | solution.py:84
  21.4 1.9 %maximum_select_fusion = bf16[8,4,64,320]{3,2,1,0:T(8,128)(2,1)} fusion(bf16[8,4,64,128]{3,2,1,0:T(8,128)(2,1)S(1)} %broadcast_select_fusion.1, bf16[8,4,64,192]{3,2,1,0:T(8,128)(2,1)S(1)} %broadcast_select_fusion, pred[8,4]{1,0:T(8,128)(4,1)S(1)} %copy.38), kind=kLoop, calls=%fused_computation.20 | loop fusion | flops 3276800 | bytes 2621472 | tf_op jit(solution)/shard_map/jit(_where)/select_n | solution.py:88
  23.3 6.9 %all-to-all-start = ((bf16[8,4,64,320]{3,2,1,0:T(8,128)(2,1)}), bf16[8,4,64,320]{3,2,1,0:T(8,128)(2,1)S(1)}, u32[]{:S(2)}, u32[]{:S(2)}) async-start(bf16[8,4,64,320]{3,2,1,0:T(8,128)(2,1)} %maximum_select_fusion), calls=%async_computation | async-start | bytes 3145728 | tf_op jit(solution)/shard_map/all_to_all | solution.py:89
  30.3 43.9 %all-gather.1 = bf16[1,512,128]{2,1,0:T(8,128)(2,1)} all-gather(bf16[1,64,128]{2,1,0:T(8,128)(2,1)S(1)} %copy-done.5), channel_id=3, replica_groups=mesh['grp'=4,'seq'=8] {'seq'}, dimensions={1}, use_global_device_ids=true | all-gather | bytes 147456 | tf_op jit(solution)/shard_map/all_gather | solution.py:91
  74.4 1.8 %copy.36 = bf16[128,16,192]{2,1,0:T(8,128)(2,1)S(1)} copy(bf16[128,16,192]{0,2,1:T(8,128)(2,1)} %param.9) | data formatting | bytes 1572864 | tf_op args[0]
  76.3 14.4 %all-gather = bf16[1,512,192]{2,1,0:T(8,128)(2,1)S(1)} all-gather(bf16[1,64,192]{2,1,0:T(8,128)(2,1)S(1)} %copy-done.4), channel_id=2, replica_groups=mesh['grp'=4,'seq'=8] {'seq'}, dimensions={1}, use_global_device_ids=true | all-gather | bytes 221184 | tf_op jit(solution)/shard_map/all_gather | solution.py:90
  90.7 0.8 fusion.47
  91.5 0.6 fusion.6
  92.4 2.1 %fusion.8 = f32[2048,128]{1,0:T(8,128)} fusion(f32[2048,512]{0,1:T(8,128)S(1)} %get-tuple-element.49, f32[2048]{0:T(1024)S(1)} %broadcast_maximum_fusion.1, f32[2048]{0:T(1024)S(1)} %get-tuple-element.38, f32[2048]{0:T(1024)S(1)} %get-tuple-element.36, bf16[1,512,128]{2,1,0:T(8,128)(2,1)S(1)} %copy-done.3), kind=kOutput, calls=%fused_computation.16 | convolution fusion | flops 271056896 | bytes 5398528 | tf_op jit(solution)/shard_map/while/body/eval_jaxpr/dot_general | solution.py:31
  94.4 1.4 reshape.242
  96.4 1.5 %gather_fusion.2 = bf16[16,64,320]{2,1,0:T(8,128)(2,1)} fusion(bf16[8,4,64,320]{3,2,1,0:T(8,128)(2,1)S(1)} %all-to-all-done, s32[16]{0:T(128)S(1)} %fusion.42), kind=kCustom, calls=%fused_computation.2 | custom fusion | bytes 1310848 | tf_op jit(solution)/shard_map/gather | solution.py:111
  98.0 2.7 %fusion.2 = (f32[2048]{0:T(1024)S(1)}, f32[1024,2048]{1,0:T(8,128)S(1)}) fusion(s32[2048]{0:T(1024)S(1)} %le.51, s32[1024]{0:T(1024)S(1)} %add.162, bf16[2048,192]{1,0:T(8,128)(2,1)} %bitcast.89, bf16[1024,320]{1,0:T(8,128)(2,1)} %bitcast.91), kind=kOutput, calls=%fused_computation.7 | convolution fusion | flops 813692928 | bytes 9981952 | tf_op jit(solution)/shard_map/dot_general | solution.py:21
  100.7 2.4 %fusion = f32[2048]{0:T(1024)S(1)} fusion(f32[1024,2048]{1,0:T(8,128)S(1)} %get-tuple-element.47, f32[2048]{0:T(1024)S(1)} %broadcast_maximum_fusion, s32[2048]{0:T(1024)S(1)} %le.51, s32[1024]{0:T(1024)S(1)} %add.162), kind=kLoop, calls=%fused_computation.5 | loop fusion | flops 10483712 | bytes 8417280 | tf_op jit(solution)/shard_map/reduce_sum | solution.py:30
  103.2 4.6 %fusion.14 = f32[2048,128]{1,0:T(8,128)} fusion(f32[1024,2048]{1,0:T(8,128)S(1)} %get-tuple-element.47, f32[2048]{0:T(1024)S(1)} %broadcast_maximum_fusion, s32[2048]{0:T(1024)S(1)} %le.51, s32[1024]{0:T(1024)S(1)} %add.162, f32[2048]{0:T(1024)S(1)} %get-tuple-element.41, f32[2048]{0:T(1024)S(1)} %get-tuple-element.40, bf16[1024,320]{1,0:T(8,128)(2,1)} %bitcast.92), kind=kOutput, calls=%fused_computation.19 | convolution fusion | flops 547880960 | bytes 9736192 | tf_op jit(solution)/shard_map/dot_general | solution.py:31
  107.8 1.4 reshape.244
  109.5 0.3 mul.110
  109.8 6.3 %convolution_convert_fusion = bf16[128,2560]{1,0:T(8,128)(2,1)S(1)} fusion(bf16[2048,2560]{1,0:T(8,128)(2,1)} %param.16, f32[128,2048]{1,0:T(8,128)S(1)} %reshape.244, f32[16,8,16,128]{3,2,1,0:T(8,128)S(1)} %bitcast.83, f32[128,2048]{1,0:T(8,128)S(1)} %reshape.242, f32[16,8,16,128]{3,2,1,0:T(8,128)S(1)} %bitcast.82), kind=kOutput, calls=%fused_computation.14 | convolution fusion | flops 1343553536 | bytes 15335424 | tf_op jit(solution)/shard_map/dot_general | solution.py:126
  116.2 1.1 copy.43
  117.3 26.8 %reduce-scatter.4.cloned.1.call-done = bf16[640,128]{1,0:T(8,128)(2,1)} async-done(((bf16[2560,128]{1,0:T(8,128)(2,1)}), bf16[640,128]{1,0:T(8,128)(2,1)}) %reduce-scatter.4.cloned.1.call-update) | async-done | bytes 163856
  144.1 1.7 %copy.44 = bf16[128,640]{1,0:T(8,128)(2,1)} copy(bf16[128,640]{0,1:T(8,128)(2,1)} %bitcast.93) | data formatting | bytes 327680
  (48 shorter events, 2.9 us)
Async XLA Ops:
  6.5 89.3 %copy-start = (bf16[128,2560]{1,0:T(8,128)(2,1)S(1)}, bf16[128,2560]{1,0:T(8,128)(2,1)}, u32[]{:S(2)}) copy-start(bf16[128,2560]{1,0:T(8,128)(2,1)} %param.14) | copy-start | bytes 1966084
  21.1 9.1 %copy-start.5 = (bf16[1,64,128]{2,1,0:T(8,128)(2,1)S(1)}, bf16[1,64,128]{2,1,0:T(8,128)(2,1)}, u32[]{:S(2)}) copy-start(bf16[1,64,128]{2,1,0:T(8,128)(2,1)} %param.13) | copy-start | bytes 49156
  21.4 54.9 %copy-start.4 = (bf16[1,64,192]{2,1,0:T(8,128)(2,1)S(1)}, bf16[1,64,192]{2,1,0:T(8,128)(2,1)}, u32[]{:S(2)}) copy-start(bf16[1,64,192]{2,1,0:T(8,128)(2,1)} %param.12) | copy-start | bytes 73732
  23.3 73.1 %all-to-all-start = ((bf16[8,4,64,320]{3,2,1,0:T(8,128)(2,1)}), bf16[8,4,64,320]{3,2,1,0:T(8,128)(2,1)S(1)}, u32[]{:S(2)}, u32[]{:S(2)}) async-start(bf16[8,4,64,320]{3,2,1,0:T(8,128)(2,1)} %maximum_select_fusion), calls=%async_computation | async-start | bytes 3145728 | tf_op jit(solution)/shard_map/all_to_all | solution.py:89
  30.2 113.9 %reduce-scatter.4.cloned.1.call-start = ((), (), s32[]{:S(2)}) async-start(), calls=%async_computation.2 | async-start | bytes 819200
  76.3 15.9 %copy-start.1 = (bf16[128,16,192]{2,1,0:T(8,128)(2,1)}, bf16[128,16,192]{2,1,0:T(8,128)(2,1)S(1)}, u32[]{:S(2)}) copy-start(bf16[128,16,192]{2,1,0:T(8,128)(2,1)S(1)} %copy.36) | copy-start | bytes 2359300
  91.5 0.9 copy-start.3
  92.4 3.5 %copy-start.2 = (bf16[1,2560,32]{1,2,0:T(8,128)(2,1)S(1)}, bf16[1,2560,32]{1,2,0:T(8,128)(2,1)}, u32[]{:S(2)}) copy-start(bf16[1,2560,32]{1,2,0:T(8,128)(2,1)} %param.15) | copy-start | bytes 491524
  92.4 4.0 %copy-start.6 = (s32[1,1,16]{2,1,0:T(1,128)S(1)}, s32[1,1,16]{2,1,0:T(1,128)}, u32[]{:S(2)}) copy-start(s32[1,1,16]{2,1,0:T(1,128)} %param.17) | copy-start | bytes 196
Sparse Core Ops, SparseCore 0:
  117.4 26.6 reduce-scatter.3
where the time goes:
time: 155 us; the launch traced here: 153 us
  blocking collectives  67.6 us (44%)
  waiting for transfers between devices  26.9 us (17%)
  matrix products  16.8 us (11%)
  local copies, waits for them, and re-layouts  14 us (9%)
  between operations  13.6 us (9%)
  starting transfers between devices  6.9 us (4%)
  other arithmetic  6.8 us (4%)
    all_gather x1, blocking collectives, shards(): piece_values = lax.all_gather(coarse_values[0], 'seq', axis=0, tiled=True)  43.9 us
    unnamed x2, waiting for transfers between devices  26.8 us
    all_gather x1, blocking collectives, shards(): piece_keys = lax.all_gather(coarse_keys[0], 'seq', axis=0, tiled=True)  14.4 us
    all_gather x1, blocking collectives, shards(): requests = lax.all_gather(selected[0], 'seq', axis=0, tiled=True)  9.31 us
    all_to_all x1, starting transfers between devices, shards(): lax.all_to_all(outgoing, 'seq', split_axis=0, concat_axis=0, tiled=True)  6.9 us
    dot_general x2, matrix products, online_block(): jnp.dot(weights.astype(jnp.bfloat16), part_values, preferred_element_type...  6.69 us
    dot_general x1, matrix products, shards(): jnp.dot(attended, out_weight, preferred_element_type=jnp.float32)  6.32 us
    unnamed x18, local copies, waits for them, and re-layouts  6.06 us
  transfers between devices with their start and end apart: 2, of which 1 were waited for; matrix products, arithmetic and copies ran while one was open for 5% of the time, Pallas kernels for 0%

commit v1 on v0

v1 whole, which is shorter than its diff:
```python
import functools
import math

import jax
import jax.numpy as jnp
from jax import lax
from jax.experimental import pallas as pl
from jax.experimental.pallas import tpu as pltpu
from jax.sharding import PartitionSpec as P

BLK = 64
SEL = 16
TILE = 128
CSTRIDE = 16
CLEN = 32

NEGATIVE = -1e30
FAR = 1 << 28
ROWS = 256
MESH = pl.DeviceIdType.MESH
HALF = BLK // 2
UNIT = BLK + HALF + BLK


def pack(keys, values, width):
    tail = keys[:, 128:width]
    folded = jnp.concatenate([tail[:HALF], tail[HALF:]], axis=1)
    return jnp.concatenate([keys[:, :128], folded, values], axis=0)


def unpack(block):
    folded = block[BLK : BLK + HALF]
    low = lax.broadcasted_iota(jnp.int32, folded.shape, 1) < 64
    zero = jnp.zeros_like(folded)
    tails = jnp.concatenate([jnp.where(low, folded, zero), jnp.where(low, zero, folded)], axis=0)
    keys = jnp.concatenate([block[:BLK], tails], axis=1)
    values = block[BLK + HALF :]
    return keys, jnp.concatenate([values, jnp.ones_like(values)], axis=1)


def kernel(
    n,
    groups,
    cap,
    scale,
    table_smem,
    table_ref,
    kpos_ref,
    query_ref,
    key_ref,
    value_ref,
    ckey_ref,
    cvalue_ref,
    hidden_ref,
    gate_ref,
    weight_ref,
    out_ref,
    packed,
    query_wide,
    tables,
    tables_smem,
    outgoing,
    incoming,
    coarse,
    keys_wide,
    values_wide,
    running,
    picked_sum,
    coarse_sum,
    attended,
    weights,
    partial,
    arrived,
    own_part,
    weight_sem,
    local_sem,
    table_send,
    table_recv,
    slot_send,
    slot_recv,
    coarse_send,
    coarse_recv,
    pass_send,
    pass_recv,
    part_send,
    part_recv,
):
    me = lax.axis_index("seq")
    group = lax.axis_index("grp")
    core = lax.rem(me, 2)
    sibling = me + 1 - 2 * core
    rows = query_ref.shape[0]
    width = query_ref.shape[1]
    heads = rows // TILE
    blocks = key_ref.shape[0]
    columns = out_ref.shape[1]
    context = blocks * BLK * n

    def weight_copy(step):
        target = lax.rem(group + step, groups)
        return pltpu.make_async_copy(
            weight_ref.at[:, pl.ds(pl.multiple_of(target * columns, 128), columns)],
            weights.at[step],
            weight_sem.at[step],
        )

    for step in range(groups):
        weight_copy(step).start()

    barrier = pltpu.get_barrier_semaphore()

    def greet(step, carry):
        pl.semaphore_signal(
            barrier, inc=1, device_id={"seq": lax.rem(me + step, n)}, device_id_type=MESH
        )
        return carry

    lax.fori_loop(1, n, greet, 0)
    for step in range(1, groups):
        pl.semaphore_signal(
            barrier, inc=1, device_id={"grp": lax.rem(group + step, groups)}, device_id_type=MESH
        )

    coarse[me] = pack(ckey_ref[...], cvalue_ref[...], width)

    def pack_one(index, carry):
        packed[index] = pack(key_ref[index], value_ref[index], width)
        return carry

    lax.fori_loop(0, blocks, pack_one, 0)
    pl.semaphore_wait(barrier, n - 1 + groups - 1)

    def table_copy(step):
        return pltpu.make_async_remote_copy(
            src_ref=table_ref,
            dst_ref=tables.at[step],
            send_sem=table_send.at[step],
            recv_sem=table_recv.at[step],
            device_id={"seq": lax.rem(me + step, n)},
            device_id_type=MESH,
        )

    def coarse_copy(step):
        return pltpu.make_async_remote_copy(
            src_ref=coarse.at[me],
            dst_ref=coarse.at[me],
            send_sem=coarse_send.at[step],
            recv_sem=coarse_recv.at[step],
            device_id={"seq": lax.rem(me + 2 * step, n)},
            device_id_type=MESH,
        )

    def pass_copy(step):
        origin = lax.rem(me - 2 * step + n, n)
        return pltpu.make_async_remote_copy(
            src_ref=coarse.at[origin],
            dst_ref=coarse.at[origin],
            send_sem=pass_send.at[step],
            recv_sem=pass_recv.at[step],
            device_id={"seq": sibling},
            device_id_type=MESH,
        )

    def slot_copy(step):
        return pltpu.make_async_remote_copy(
            src_ref=outgoing.at[step],
            dst_ref=incoming.at[step],
            send_sem=slot_send.at[step],
            recv_sem=slot_recv.at[step],
            device_id={"seq": lax.rem(me + step, n)},
            device_id_type=MESH,
        )

    def send_table(step, carry):
        table_copy(step).start()
        return carry

    lax.fori_loop(1, n, send_table, 0)

    def send_coarse(step, carry):
        coarse_copy(step).start()
        return carry

    lax.fori_loop(1, n // 2, send_coarse, 0)
    pass_copy(0).start()

    for slot in range(cap):
        incoming[0, slot] = packed[table_smem[0, me * cap + slot]]
    main = query_ref[:, :128]
    tail = query_ref[:, 128:width]
    query_wide[:, :128] = main
    query_wide[:, 128:] = jnp.concatenate([tail, tail], axis=1)

    def wait_table(step, carry):
        table_copy(step).wait_recv()
        return carry

    lax.fori_loop(1, n, wait_table, 0)
    to_smem = pltpu.make_async_copy(tables, tables_smem, local_sem)
    to_smem.start()
    to_smem.wait()

    def send_slots(index, carry):
        step = n // 2 + index
        for slot in range(cap):
            outgoing[step, slot] = packed[tables_smem[n - step, 0, me * cap + slot]]
        slot_copy(step).start()
        return carry

    lax.fori_loop(0, n // 2, send_slots, 0)

    def send_slots_low(index, carry):
        step = n // 2 - 1 - index
        for slot in range(cap):
            outgoing[step, slot] = packed[tables_smem[n - step, 0, me * cap + slot]]
        slot_copy(step).start()
        return carry

    lax.fori_loop(0, n // 2 - 1, send_slots_low, 0)

    first_pos = context - TILE * n + me * TILE

    def attend(kpos, width_keys, total, first):
        relative = kpos - first_pos
        offsets = lax.broadcasted_iota(jnp.int32, (ROWS, width_keys), 0) // heads

        def chunk(index, carry):
            at = pl.multiple_of(index * ROWS, ROWS)
            here = pl.ds(at, ROWS)
            scores = lax.dot_general(
                query_wide[here, :],
                keys_wide[:width_keys],
                (((1,), (1,)), ((), ())),
                preferred_element_type=jnp.float32,
            )
            seen = relative - index * (ROWS // heads) <= offsets
            scores = jnp.where(seen, scores, -jnp.inf)
            top = jnp.max(scores, axis=1, keepdims=True)
            old = jnp.where(first, jnp.full((ROWS, 128), NEGATIVE, jnp.float32), running[here, :])
            new = jnp.maximum(old, top)
            factor = jnp.exp2((old - new) * scale)
            exponents = jnp.exp2((scores - new[:, :1]) * scale).astype(jnp.bfloat16)
            added = jnp.dot(
                exponents, values_wide[:width_keys], preferred_element_type=jnp.float32
            )
            for part in range(2):
                before = total[part, here, :]
                before = jnp.where(first, jnp.zeros_like(before), before)
                total[part, here, :] = before * factor + added[:, part * 128 : part * 128 + 128]
            running[here, :] = new
            return carry

        lax.fori_loop(0, rows // ROWS, chunk, 0)

    gates = jax.nn.sigmoid(
        jnp.dot(hidden_ref[...], gate_ref[...], preferred_element_type=jnp.float32)
    )

    def forward(step, carry):
        coarse_copy(step).wait_recv()
        pass_copy(step).start()
        return carry

    lax.fori_loop(1, n // 2, forward, 0)

    def passed(step, carry):
        pass_copy(step).wait_recv()
        return carry

    lax.fori_loop(0, n // 2, passed, 0)

    pieces = min(n, 8)

    def coarse_step(index, carry):
        for piece in range(pieces):
            keys, values = unpack(coarse[index * pieces + piece])
            keys_wide[piece * BLK : (piece + 1) * BLK] = keys
            values_wide[piece * BLK : (piece + 1) * BLK] = values
        token = lax.broadcasted_iota(jnp.int32, (1, pieces * BLK), 1) + index * (pieces * BLK)
        attend(token * CSTRIDE + CLEN - 1, pieces * BLK, coarse_sum, index == 0)
        return carry

    lax.fori_loop(0, n // pieces, coarse_step, 0)

    def picked_step(step, carry):
        @pl.when(step > 0)
        def _():
            slot_copy(jnp.maximum(step, 1)).wait_recv()

        for slot in range(cap):
            keys, values = unpack(incoming[step, slot])
            keys_wide[slot * BLK : (slot + 1) * BLK] = keys
            values_wide[slot * BLK : (slot + 1) * BLK] = values
        owner = lax.rem(me - step + n, n)
        attend(kpos_ref[owner], cap * BLK, picked_sum, step == 0)
        return carry

    lax.fori_loop(0, n, picked_step, 0)

    for head in range(heads):
        mine = pl.ds(head, TILE, stride=heads)
        of_coarse = coarse_sum[0, mine, :] / coarse_sum[1, mine, :]
        of_picked = picked_sum[0, mine, :] / picked_sum[1, mine, :]
        mixed = gates[:, head : head + 1] * of_coarse + gates[:, heads + head : heads + head + 1] * of_picked
        attended[:, head * 128 : (head + 1) * 128] = mixed.astype(jnp.bfloat16)

    def part_copy(step):
        return pltpu.make_async_remote_copy(
            src_ref=partial.at[step],
            dst_ref=arrived.at[step],
            send_sem=part_send.at[step],
            recv_sem=part_recv.at[step],
            device_id={"grp": lax.rem(group + step, groups)},
            device_id_type=MESH,
        )

    for step in range(1, groups):
        weight_copy(step).wait()
        partial[step] = jnp.dot(
            attended[...], weights[step], preferred_element_type=jnp.float32
        ).astype(jnp.bfloat16)
        part_copy(step).start()
    weight_copy(0).wait()
    own_part[...] = jnp.dot(attended[...], weights[0], preferred_element_type=jnp.float32)

    def sent(step, carry):
        table_copy(step).wait_send()
        slot_copy(step).wait_send()
        return carry

    lax.fori_loop(1, n, sent, 0)

    def sent_coarse(step, carry):
        coarse_copy(step).wait_send()
        pass_copy(step).wait_send()
        return carry

    lax.fori_loop(1, n // 2, sent_coarse, 0)
    pass_copy(0).wait_send()
    total = own_part[...]
    for step in range(1, groups):
        part_copy(step).wait_recv()
        total = total + arrived[step].astype(jnp.float32)
    out_ref[...] = total.astype(out_ref.dtype)
    for step in range(1, groups):
        part_copy(step).wait_send()


def shards(
    queries,
    key_cache,
    group_value_cache,
    coarse_keys,
    coarse_values,
    hidden,
    gate_weight,
    out_weight,
    selected,
):
    n = lax.axis_size("seq")
    groups = lax.axis_size("grp")
    ctx_dev = key_cache.shape[1]
    heads = queries.shape[1]
    width = queries.shape[2]
    vwidth = group_value_cache.shape[2]
    rows = TILE * heads
    blocks = ctx_dev // BLK
    cap = max(1, 2 * SEL // n)
    columns = out_weight.shape[1] // groups
    pieces = min(n, 8)
    wide = max(pieces, cap) * BLK

    mine = selected[0, 0]
    owners = mine // blocks
    earlier = jnp.tril(jnp.ones((SEL, SEL), jnp.int32), -1)
    rank = jnp.sum((owners[:, None] == owners[None, :]).astype(jnp.int32) * earlier, axis=1)
    slot_ids = jnp.arange(n * cap, dtype=jnp.int32)
    match = (owners * cap + rank)[:, None] == slot_ids[None, :]
    table = jnp.max(jnp.where(match, mine[:, None], -1), axis=0)
    local = jnp.maximum(table - slot_ids // cap * blocks, 0)
    request = jnp.pad(local, (0, 128 - n * cap)).reshape(1, 128)
    kpos = jnp.where(table < 0, FAR, table * BLK)[:, None] + jnp.arange(BLK, dtype=jnp.int32)
    kpos = kpos.reshape(n, 1, cap * BLK)

    vmem = pl.BlockSpec(memory_space=pltpu.VMEM)
    dma = pltpu.SemaphoreType.DMA
    bf16, f32 = jnp.bfloat16, jnp.float32
    return pl.pallas_call(
        functools.partial(kernel, n, groups, cap, width**-0.5 * math.log2(math.e)),
        out_shape=jax.ShapeDtypeStruct((TILE, columns), bf16),
        in_specs=[pl.BlockSpec(memory_space=pltpu.SMEM)]
        + [vmem] * 9
        + [pl.BlockSpec(memory_space=pl.ANY)],
        out_specs=vmem,
        scratch_shapes=[
            pltpu.VMEM((blocks, UNIT, 128), bf16),
            pltpu.VMEM((rows, 256), bf16),
            pltpu.VMEM((n, 1, 128), jnp.int32),
            pltpu.SMEM((n, 1, 128), jnp.int32),
            pltpu.VMEM((n, cap, UNIT, 128), bf16),
            pltpu.VMEM((n, cap, UNIT, 128), bf16),
            pltpu.VMEM((n, UNIT, 128), bf16),
            pltpu.VMEM((wide, 256), bf16),
            pltpu.VMEM((wide, 256), bf16),
            pltpu.VMEM((rows, 128), f32),
            pltpu.VMEM((2, rows, 128), f32),
            pltpu.VMEM((2, rows, 128), f32),
            pltpu.VMEM((TILE, heads * vwidth), bf16),
            pltpu.VMEM((groups, heads * vwidth, columns), bf16),
            pltpu.VMEM((groups, TILE, columns), bf16),
            pltpu.VMEM((groups, TILE, columns), bf16),
            pltpu.VMEM((TILE, columns), f32),
            dma((groups,)),
            dma,
            dma((n,)),
            dma((n,)),
            dma((n,)),
            dma((n,)),
            dma((n // 2,)),
            dma((n // 2,)),
            dma((n // 2,)),
            dma((n // 2,)),
            dma((groups,)),
            dma((groups,)),
        ],
        compiler_params=pltpu.CompilerParams(
            collective_id=0, has_side_effects=True, vmem_limit_bytes=60 * 1024 * 1024
        ),
    )(
        request,
        request,
        kpos,
        queries.reshape(rows, width),
        key_cache.reshape(blocks, BLK, width),
        group_value_cache.reshape(blocks, BLK, vwidth),
        coarse_keys[0],
        coarse_values[0],
        hidden,
        gate_weight[0],
        out_weight,
    )


def solution(mesh):
    return jax.shard_map(
        shards,
        mesh=mesh,
        in_specs=(
            P("seq", "grp", None),
            P("grp", "seq", None),
            P("grp", "seq", None),
            P("grp", "seq", None),
            P("grp", "seq", None),
            P("seq", None),
            P("grp", None, None),
            P("grp", None),
            P("grp", "seq", None),
        ),
        out_specs=P("seq", "grp"),
        check_vma=False,
    )
```

time: 155 us -> 92.4 us (0.60)
  the two profiles are of different devices: /device:TPU:8 before, /device:TPU:18 now
where the time goes in v1:
time: 92.4 us; the launch traced here: 92.2 us
  Pallas kernels  80.8 us (87%)
  local copies, waits for them, and re-layouts  9.17 us (10%)
  other arithmetic  2.22 us (2%)
    pallas_call x1, Pallas kernels, shards(): pl.pallas_call(functools.partial(kernel, n, groups, cap, width ** (-0.5)...  80.8 us
    unnamed x4, local copies, waits for them, and re-layouts  8.25 us

profile of v1, /device:TPU:18, one launch (start us, length us, event | category | flops | bytes accessed | tf_op | source)
XLA Modules:
  0.0 92.2 jit_solution(10249676278019216971)
XLA Ops:
  0.0 0.7 and_select_fusion.1
  0.7 0.2 select_reduce_fusion.1
  0.9 0.7 select_reduce_fusion
  1.6 0.6 pad_bitcast_fusion.table_smem.table_ref
  2.2 0.1 add.60
  2.3 0.1 select_n.45
  2.4 0.1 add.57
  2.4 0.1 add.58
  2.5 0.6 broadcast_add_fusion.kpos_ref
  3.1 2.0 %copy.17 = bf16[1,1024,192]{2,1,0:T(8,128)(2,1)} copy(bf16[1,1024,192]{1,2,0:T(8,128)(2,1)} %param.10) | data formatting | bytes 786432 | tf_op args[1]
  5.1 2.0 %copy.18 = bf16[1,2560,32]{2,1,0:T(8,128)(2,1)} copy(bf16[1,2560,32]{1,2,0:T(8,128)(2,1)} %param.15) | data formatting | bytes 327680 | tf_op args[6]
  7.2 2.6 %copy.16 = bf16[128,16,192]{2,1,0:T(8,128)(2,1)} copy(bf16[128,16,192]{0,2,1:T(8,128)(2,1)} %param.9) | data formatting | bytes 1572864 | tf_op args[0]
  9.8 80.8 %shard_map.91 = bf16[128,640]{1,0:T(8,128)(2,1)} custom-call(s32[1,128]{1,0:T(1,128)} %pad_bitcast_fusion.table_smem.table_ref, s32[1,128]{1,0:T(1,128)} %pad_bitcast_fusion.table_smem.table_ref, s32[8,1,256]{2,1,0:T(1,128)} %broadcast_add_fusion.kpos_ref, bf16[2048,192]{1,0:T(8,128)(2,1)} %bitcast.10, bf16[16,64,192]{2,1,0:T(8,128)(2,1)} %bitcast.12, ...), custom_call_target="tpu_custom_call" | custom-call | tf_op jit(solution)/shard_map/pallas_call | solution.py:388
  90.6 1.6 %copy.20 = bf16[128,640]{1,0:T(8,128)(2,1)} copy(bf16[128,640]{1,0:T(8,128)(2,1)} %shard_map.91) | data formatting | bytes 327680
  (3 shorter events, 0.0 us)

commit v2 on v1

v2 whole, which is shorter than its diff:
```python
import functools
import math

import jax
import jax.numpy as jnp
from jax import lax
from jax.experimental import pallas as pl
from jax.experimental.pallas import tpu as pltpu
from jax.sharding import PartitionSpec as P

BLK = 64
SEL = 16
TILE = 128
CSTRIDE = 16
CLEN = 32

NEGATIVE = -1e30
FAR = 1 << 28
MESH = pl.DeviceIdType.MESH
HALF = BLK // 2
UNIT = BLK + HALF + BLK


def pack(keys, values, width):
    tail = keys[:, 128:width]
    folded = jnp.concatenate([tail[:HALF], tail[HALF:]], axis=1)
    return jnp.concatenate([keys[:, :128], folded, values], axis=0)


def unpack(block):
    folded = block[BLK : BLK + HALF]
    low = lax.broadcasted_iota(jnp.int32, folded.shape, 1) < 64
    zero = jnp.zeros_like(folded)
    tails = jnp.concatenate([jnp.where(low, folded, zero), jnp.where(low, zero, folded)], axis=0)
    return jnp.concatenate([block[:BLK], tails], axis=1), block[BLK + HALF :]


def picks(read, owner, blocks, cap):
    low = owner * blocks
    found = [jnp.int32(-1)] * cap
    count = jnp.int32(0)
    for entry in range(SEL):
        block = read(entry)
        here = (block >= low) & (block < low + blocks)
        for slot in range(cap):
            found[slot] = jnp.where(here & (count == slot), block, found[slot])
        count = count + here.astype(jnp.int32)
    return found


def kernel(
    n,
    groups,
    cap,
    scale,
    own_smem,
    own_table,
    query_hbm,
    key_hbm,
    value_hbm,
    ckey_hbm,
    cvalue_hbm,
    hidden_hbm,
    gate_hbm,
    weight_hbm,
    out_ref,
    query_ref,
    key_ref,
    value_ref,
    ckey_ref,
    cvalue_ref,
    hidden_ref,
    gate_ref,
    packed,
    query_wide,
    tables,
    tables_smem,
    outgoing,
    incoming,
    coarse,
    keys_wide,
    values_wide,
    picked_top,
    picked_sum,
    picked_out,
    coarse_top,
    coarse_sum,
    coarse_out,
    attended,
    weights,
    partial,
    arrived,
    own_part,
    input_sem,
    weight_sem,
    local_sem,
    table_send,
    table_recv,
    slot_send,
    slot_recv,
    coarse_send,
    coarse_recv,
    pass_send,
    pass_recv,
    part_send,
    part_recv,
):
    me = lax.axis_index("seq")
    group = lax.axis_index("grp")
    core = lax.rem(me, 2)
    sibling = me + 1 - 2 * core
    heads, width, _ = query_ref.shape
    blocks = value_ref.shape[0]
    columns = out_ref.shape[1]
    context = blocks * BLK * n
    span = 2 * TILE

    barrier = pltpu.get_barrier_semaphore()

    def greet(step, carry):
        pl.semaphore_signal(
            barrier, inc=1, device_id={"seq": lax.rem(me + step, n)}, device_id_type=MESH
        )
        return carry

    lax.fori_loop(1, n, greet, 0)
    for step in range(1, groups):
        pl.semaphore_signal(
            barrier, inc=1, device_id={"grp": lax.rem(group + step, groups)}, device_id_type=MESH
        )

    loads = [
        pltpu.make_async_copy(source, target, input_sem.at[index])
        for index, (source, target) in enumerate(
            [
                (ckey_hbm, ckey_ref),
                (cvalue_hbm, cvalue_ref),
                (key_hbm, key_ref),
                (value_hbm, value_ref),
                (query_hbm, query_ref),
                (hidden_hbm, hidden_ref),
                (gate_hbm, gate_ref),
            ]
        )
    ]
    for load in loads:
        load.start()

    def weight_copy(step):
        target = lax.rem(group + step, groups)
        return pltpu.make_async_copy(
            weight_hbm.at[:, pl.ds(pl.multiple_of(target * columns, 128), columns)],
            weights.at[step],
            weight_sem.at[step],
        )

    for step in range(groups):
        weight_copy(step).start()

    loads[0].wait()
    loads[1].wait()
    coarse[me] = pack(ckey_ref[...], cvalue_ref[...], width)
    loads[2].wait()
    loads[3].wait()
    for pair in range(blocks // 2):
        both = key_ref[:, pair * 128 : (pair + 1) * 128].T
        packed[2 * pair] = pack(both[:BLK], value_ref[2 * pair], width)
        packed[2 * pair + 1] = pack(both[BLK:], value_ref[2 * pair + 1], width)
    pl.semaphore_wait(barrier, n - 1 + groups - 1)

    def table_copy(step):
        return pltpu.make_async_remote_copy(
            src_ref=own_table,
            dst_ref=tables.at[step],
            send_sem=table_send.at[step],
            recv_sem=table_recv.at[step],
            device_id={"seq": lax.rem(me + step, n)},
            device_id_type=MESH,
        )

    def coarse_copy(step):
        return pltpu.make_async_remote_copy(
            src_ref=coarse.at[me],
            dst_ref=coarse.at[me],
            send_sem=coarse_send.at[step],
            recv_sem=coarse_recv.at[step],
            device_id={"seq": lax.rem(me + 2 * step, n)},
            device_id_type=MESH,
        )

    def pass_copy(step):
        origin = lax.rem(me - 2 * step + n, n)
        return pltpu.make_async_remote_copy(
            src_ref=coarse.at[origin],
            dst_ref=coarse.at[origin],
            send_sem=pass_send.at[step],
            recv_sem=pass_recv.at[step],
            device_id={"seq": sibling},
            device_id_type=MESH,
        )

    def slot_copy(step):
        return pltpu.make_async_remote_copy(
            src_ref=outgoing.at[step],
            dst_ref=incoming.at[step],
            send_sem=slot_send.at[step],
            recv_sem=slot_recv.at[step],
            device_id={"seq": lax.rem(me + step, n)},
            device_id_type=MESH,
        )

    def turn(index):
        return n // 2 + (index // 2) * (1 - 2 * lax.rem(index, 2))

    def send_table(step, carry):
        table_copy(step).start()
        return carry

    lax.fori_loop(1, n, send_table, 0)

    def send_coarse(step, carry):
        coarse_copy(step).start()
        return carry

    lax.fori_loop(1, n // 2, send_coarse, 0)
    pass_copy(0).start()

    def wait_table(step, carry):
        table_copy(step).wait_recv()
        return carry

    lax.fori_loop(1, n, wait_table, 0)
    to_smem = pltpu.make_async_copy(tables, tables_smem, local_sem)
    to_smem.start()
    to_smem.wait()

    def send_slots(index, carry):
        step = turn(index)
        wanted = picks(lambda entry: tables_smem[n - step, 0, 0, entry], me, blocks, cap)
        for slot in range(cap):
            outgoing[step, slot] = packed[jnp.maximum(wanted[slot] - me * blocks, 0)]
        slot_copy(step).start()
        return carry

    lax.fori_loop(1, n, send_slots, 0)

    loads[4].wait()
    for head in range(heads):
        one = query_ref[head]
        query_wide[:width, head * 128 : (head + 1) * 128] = one
        query_wide[width:, head * 128 : (head + 1) * 128] = one[128:]

    first_pos = context - TILE * n + me * TILE
    row = lax.broadcasted_iota(jnp.int32, (BLK, span), 0)
    query = lax.rem(lax.broadcasted_iota(jnp.int32, (BLK, span), 1), TILE)

    def fill(place, block):
        keys, values = unpack(block)
        keys_wide[place * BLK : (place + 1) * BLK] = keys
        return values

    def attend(count, bounds, stride, top_ref, sum_ref, out, first):
        lag = row * stride - query

        def chunk(index, carry):
            here = pl.ds(pl.multiple_of(index * span, span), span)
            scores = jnp.dot(
                keys_wide[: count * BLK], query_wide[:, here], preferred_element_type=jnp.float32
            )
            scores = jnp.concatenate(
                [
                    jnp.where(lag <= bounds[block], scores[block * BLK : (block + 1) * BLK], -jnp.inf)
                    for block in range(count)
                ],
                axis=0,
            )
            top = jnp.max(scores, axis=0, keepdims=True)
            if first:
                new = jnp.maximum(top, NEGATIVE)
            else:
                old = top_ref[:, here]
                new = jnp.maximum(old, top)
                factor = jnp.exp2((old - new) * scale)
            exponents = jnp.exp2((scores - new) * scale).astype(jnp.bfloat16)
            added = jnp.dot(
                values_wide[:, : count * BLK], exponents, preferred_element_type=jnp.float32
            )
            if first:
                out[:, here] = added[:128]
                sum_ref[:, here] = added[128:129]
            else:
                out[:, here] = out[:, here] * factor + added[:128]
                sum_ref[:, here] = sum_ref[:, here] * factor + added[128:129]
            top_ref[:, here] = new
            return carry

        lax.fori_loop(0, heads * TILE // span, chunk, 0, unroll=4)

    values_wide[128:, :] = jnp.ones_like(values_wide[128:, :])

    def attend_picked(owner, group_of, first):
        wanted = picks(lambda entry: own_smem[0, 0, entry], owner, blocks, cap)
        values = [fill(slot, group_of[slot]) for slot in range(cap)]
        values_wide[:128, : cap * BLK] = jnp.concatenate(values, axis=0).T
        bounds = [
            jnp.where(wanted[slot] < 0, -FAR, first_pos - wanted[slot] * BLK) for slot in range(cap)
        ]
        attend(cap, bounds, 1, picked_top, picked_sum, picked_out, first)

    mine = picks(lambda entry: own_smem[0, 0, entry], me, blocks, cap)
    attend_picked(me, [packed[jnp.maximum(block - me * blocks, 0)] for block in mine], True)

    loads[5].wait()
    loads[6].wait()
    gates = jax.nn.sigmoid(
        lax.dot_general(
            gate_ref[...],
            hidden_ref[...],
            (((1,), (1,)), ((), ())),
            preferred_element_type=jnp.float32,
        )
    )

    def forward(step, carry):
        coarse_copy(step).wait_recv()
        pass_copy(step).start()
        return carry

    lax.fori_loop(1, n // 2, forward, 0)

    def passed(step, carry):
        pass_copy(step).wait_recv()
        return carry

    lax.fori_loop(0, n // 2, passed, 0)

    pieces = min(n, 8)

    def coarse_step(index, first):
        values = [fill(piece, coarse[index * pieces + piece]) for piece in range(pieces)]
        values_wide[:128, : pieces * BLK] = jnp.concatenate(values, axis=0).T
        start = first_pos - (CLEN - 1) - index * (pieces * BLK * CSTRIDE)
        bounds = [start - piece * (BLK * CSTRIDE) for piece in range(pieces)]
        attend(pieces, bounds, CSTRIDE, coarse_top, coarse_sum, coarse_out, first)

    coarse_step(0, True)
    if n > pieces:

        def coarse_more(index, carry):
            coarse_step(index, False)
            return carry

        lax.fori_loop(1, n // pieces, coarse_more, 0)

    def picked_step(index, carry):
        step = turn(index)
        slot_copy(step).wait_recv()
        owner = lax.rem(me - step + n, n)
        attend_picked(owner, [incoming[step, slot] for slot in range(cap)], False)
        return carry

    lax.fori_loop(1, n, picked_step, 0)

    for head in range(heads):
        here = slice(head * 128, (head + 1) * 128)
        of_coarse = gates[head : head + 1] / coarse_sum[:, here]
        of_picked = gates[heads + head : heads + head + 1] / picked_sum[:, here]
        mixed = coarse_out[:, here] * of_coarse + picked_out[:, here] * of_picked
        attended[:, here] = mixed.T.astype(jnp.bfloat16)

    def part_copy(step):
        return pltpu.make_async_remote_copy(
            src_ref=partial.at[step],
            dst_ref=arrived.at[step],
            send_sem=part_send.at[step],
            recv_sem=part_recv.at[step],
            device_id={"grp": lax.rem(group + step, groups)},
            device_id_type=MESH,
        )

    for step in range(1, groups):
        weight_copy(step).wait()
        partial[step] = jnp.dot(
            attended[...], weights[step], preferred_element_type=jnp.float32
        ).astype(jnp.bfloat16)
        part_copy(step).start()
    weight_copy(0).wait()
    own_part[...] = jnp.dot(attended[...], weights[0], preferred_element_type=jnp.float32)

    def sent(step, carry):
        table_copy(step).wait_send()
        slot_copy(step).wait_send()
        return carry

    lax.fori_loop(1, n, sent, 0)

    def sent_coarse(step, carry):
        coarse_copy(step).wait_send()
        pass_copy(step).wait_send()
        return carry

    lax.fori_loop(1, n // 2, sent_coarse, 0)
    pass_copy(0).wait_send()
    total = own_part[...]
    for step in range(1, groups):
        part_copy(step).wait_recv()
        total = total + arrived[step].astype(jnp.float32)
    out_ref[...] = total.astype(out_ref.dtype)
    for step in range(1, groups):
        part_copy(step).wait_send()


def shards(
    queries,
    key_cache,
    group_value_cache,
    coarse_keys,
    coarse_values,
    hidden,
    gate_weight,
    out_weight,
    selected,
):
    n = lax.axis_size("seq")
    groups = lax.axis_size("grp")
    ctx_dev = key_cache.shape[1]
    heads = queries.shape[1]
    width = queries.shape[2]
    vwidth = group_value_cache.shape[2]
    rows = TILE * heads
    blocks = ctx_dev // BLK
    cap = max(1, 2 * SEL // n)
    columns = out_weight.shape[1] // groups
    pieces = min(n, 8)
    wide = max(pieces, cap) * BLK

    vmem = pl.BlockSpec(memory_space=pltpu.VMEM)
    hbm = pl.BlockSpec(memory_space=pl.ANY)
    dma = pltpu.SemaphoreType.DMA
    bf16, f32 = jnp.bfloat16, jnp.float32
    inputs = (
        queries.transpose(1, 2, 0),
        key_cache[0].T,
        group_value_cache.reshape(blocks, BLK, vwidth),
        coarse_keys[0],
        coarse_values[0],
        hidden,
        gate_weight[0].T,
    )
    return pl.pallas_call(
        functools.partial(kernel, n, groups, cap, width**-0.5 * math.log2(math.e)),
        out_shape=jax.ShapeDtypeStruct((TILE, columns), bf16),
        in_specs=[pl.BlockSpec(memory_space=pltpu.SMEM), vmem] + [hbm] * (len(inputs) + 1),
        out_specs=vmem,
        scratch_shapes=[pltpu.VMEM(one.shape, bf16) for one in inputs]
        + [
            pltpu.VMEM((blocks, UNIT, 128), bf16),
            pltpu.VMEM((256, rows), bf16),
            pltpu.VMEM((n, 1, 1, SEL), jnp.int32),
            pltpu.SMEM((n, 1, 1, SEL), jnp.int32),
            pltpu.VMEM((n, cap, UNIT, 128), bf16),
            pltpu.VMEM((n, cap, UNIT, 128), bf16),
            pltpu.VMEM((n, UNIT, 128), bf16),
            pltpu.VMEM((wide, 256), bf16),
            pltpu.VMEM((144, wide), bf16),
            pltpu.VMEM((1, rows), f32),
            pltpu.VMEM((1, rows), f32),
            pltpu.VMEM((vwidth, rows), f32),
            pltpu.VMEM((1, rows), f32),
            pltpu.VMEM((1, rows), f32),
            pltpu.VMEM((vwidth, rows), f32),
            pltpu.VMEM((TILE, heads * vwidth), bf16),
            pltpu.VMEM((groups, heads * vwidth, columns), bf16),
            pltpu.VMEM((groups, TILE, columns), bf16),
            pltpu.VMEM((groups, TILE, columns), bf16),
            pltpu.VMEM((TILE, columns), f32),
            dma((len(inputs),)),
            dma((groups,)),
            dma,
            dma((n,)),
            dma((n,)),
            dma((n,)),
            dma((n,)),
            dma((n // 2,)),
            dma((n // 2,)),
            dma((n // 2,)),
            dma((n // 2,)),
            dma((groups,)),
            dma((groups,)),
        ],
        compiler_params=pltpu.CompilerParams(
            collective_id=0, has_side_effects=True, vmem_limit_bytes=60 * 1024 * 1024
        ),
    )(selected, selected, *inputs, out_weight)


def solution(mesh):
    return jax.shard_map(
        shards,
        mesh=mesh,
        in_specs=(
            P("seq", "grp", None),
            P("grp", "seq", None),
            P("grp", "seq", None),
            P("grp", "seq", None),
            P("grp", "seq", None),
            P("seq", None),
            P("grp", None, None),
            P("grp", None),
            P("grp", "seq", None),
        ),
        out_specs=P("seq", "grp"),
        check_vma=False,
    )
```

time: 92.4 us -> 63.2 us (0.68)
  the two profiles are of different devices: /device:TPU:18 before, /device:TPU:0 now
where the time goes in v2:
time: 63.2 us; the launch traced here: 63.1 us
  Pallas kernels  61.5 us (97%)
  local copies, waits for them, and re-layouts  1.6 us (3%)
    pallas_call x1, Pallas kernels, shards(): pl.pallas_call(functools.partial(kernel, n, groups, cap, width ** (-0.5)...  61.5 us
    unnamed x1, local copies, waits for them, and re-layouts  1.6 us

profile of v2, /device:TPU:0, one launch (start us, length us, event | category | flops | bytes accessed | tf_op | source)
XLA Modules:
  0.0 63.1 jit_solution(4050571035718405222)
XLA Ops:
  0.0 61.5 %shard_map.91 = bf16[128,640]{1,0:T(8,128)(2,1)} custom-call(s32[1,1,16]{2,1,0:T(1,128)} %own_table.1, s32[1,1,16]{2,1,0:T(1,128)} %own_table.1, bf16[16,192,128]{2,1,0:T(8,128)(2,1)} %bitcast.10, bf16[192,1024]{1,0:T(8,128)(2,1)} %bitcast.11, bf16[16,64,128]{2,1,0:T(8,128)(2,1)} %bitcast.12, bf16[64,192]{1,0:T(8,128)(2,1)} %bitcast.14, ...), custom_call_target="tpu_custom_call" | custom-call | tf_op jit(solution)/shard_map/pallas_call | solution.py:450
  61.5 1.6 %copy.11 = bf16[128,640]{1,0:T(8,128)(2,1)} copy(bf16[128,640]{1,0:T(8,128)(2,1)} %shard_map.91) | data formatting | bytes 327680

commit v3 on v2

--- a/solution.py
+++ b/solution.py
@@ -33,6 +33,15 @@
     zero = jnp.zeros_like(folded)
     tails = jnp.concatenate([jnp.where(low, folded, zero), jnp.where(low, zero, folded)], axis=0)
     return jnp.concatenate([block[:BLK], tails], axis=1), block[BLK + HALF :]
+
+
+def flip(index, step, size):
+    shared = 0
+    bit = 1
+    while bit < size:
+        shared = shared + lax.rem(index // bit, 2) * (step // bit % 2) * bit
+        bit *= 2
+    return index + step - 2 * shared
 
 
 def picks(read, owner, blocks, cap):
@@ -119,14 +128,14 @@
 
     def greet(step, carry):
         pl.semaphore_signal(
-            barrier, inc=1, device_id={"seq": lax.rem(me + step, n)}, device_id_type=MESH
+            barrier, inc=1, device_id={"seq": flip(me, step, n)}, device_id_type=MESH
         )
         return carry
 
     lax.fori_loop(1, n, greet, 0)
     for step in range(1, groups):
         pl.semaphore_signal(
-            barrier, inc=1, device_id={"grp": lax.rem(group + step, groups)}, device_id_type=MESH
+            barrier, inc=1, device_id={"grp": flip(group, step, groups)}, device_id_type=MESH
         )
 
     loads = [
@@ -147,14 +156,14 @@
         load.start()
 
     def weight_copy(step):
-        target = lax.rem(group + step, groups)
+        target = flip(group, step, groups)
         return pltpu.make_async_copy(
             weight_hbm.at[:, pl.ds(pl.multiple_of(target * columns, 128), columns)],
             weights.at[step],
             weight_sem.at[step],
         )
 
-    for step in range(groups):
+    for step in reversed(range(groups)):
         weight_copy(step).start()
 
     loads[0].wait()
@@ -174,7 +183,7 @@
             dst_ref=tables.at[step],
             send_sem=table_send.at[step],
             recv_sem=table_recv.at[step],
-            device_id={"seq": lax.rem(me + step, n)},
+            device_id={"seq": flip(me, step, n)},
             device_id_type=MESH,
         )
 
@@ -184,12 +193,12 @@
             dst_ref=coarse.at[me],
             send_sem=coarse_send.at[step],
             recv_sem=coarse_recv.at[step],
-            device_id={"seq": lax.rem(me + 2 * step, n)},
+            device_id={"seq": flip(me, 2 * step, n)},
             device_id_type=MESH,
         )
 
     def pass_copy(step):
-        origin = lax.rem(me - 2 * step + n, n)
+        origin = flip(me, 2 * step, n)
         return pltpu.make_async_remote_copy(
             src_ref=coarse.at[origin],
             dst_ref=coarse.at[origin],
@@ -205,12 +214,9 @@
             dst_ref=incoming.at[step],
             send_sem=slot_send.at[step],
             recv_sem=slot_recv.at[step],
-            device_id={"seq": lax.rem(me + step, n)},
+            device_id={"seq": flip(me, step, n)},
             device_id_type=MESH,
         )
-
-    def turn(index):
-        return n // 2 + (index // 2) * (1 - 2 * lax.rem(index, 2))
 
     def send_table(step, carry):
         table_copy(step).start()
@@ -234,9 +240,8 @@
     to_smem.start()
     to_smem.wait()
 
-    def send_slots(index, carry):
-        step = turn(index)
-        wanted = picks(lambda entry: tables_smem[n - step, 0, 0, entry], me, blocks, cap)
+    def send_slots(step, carry):
+        wanted = picks(lambda entry: tables_smem[step, 0, 0, entry], me, blocks, cap)
         for slot in range(cap):
             outgoing[step, slot] = packed[jnp.maximum(wanted[slot] - me * blocks, 0)]
         slot_copy(step).start()
@@ -352,10 +357,9 @@
 
         lax.fori_loop(1, n // pieces, coarse_more, 0)
 
-    def picked_step(index, carry):
-        step = turn(index)
+    def picked_step(step, carry):
         slot_copy(step).wait_recv()
-        owner = lax.rem(me - step + n, n)
+        owner = flip(me, step, n)
         attend_picked(owner, [incoming[step, slot] for slot in range(cap)], False)
         return carry
 
@@ -374,11 +378,11 @@
             dst_ref=arrived.at[step],
             send_sem=part_send.at[step],
             recv_sem=part_recv.at[step],
-            device_id={"grp": lax.rem(group + step, groups)},
+            device_id={"grp": flip(group, step, groups)},
             device_id_type=MESH,
         )
 
-    for step in range(1, groups):
+    for step in reversed(range(1, groups)):
         weight_copy(step).wait()
         partial[step] = jnp.dot(
             attended[...], weights[step], preferred_element_type=jnp.float32

time: 63.2 us -> 54.7 us (0.87)
  the two profiles are of different devices: /device:TPU:0 before, /device:TPU:8 now
where the time goes in v3:
time: 54.7 us; the launch traced here: 54.5 us
  Pallas kernels  52.9 us (97%)
  local copies, waits for them, and re-layouts  1.6 us (3%)
    pallas_call x1, Pallas kernels, shards(): pl.pallas_call(functools.partial(kernel, n, groups, cap, width ** (-0.5)...  52.9 us
    unnamed x1, local copies, waits for them, and re-layouts  1.6 us

profile of v3, /device:TPU:8, one launch (start us, length us, event | category | flops | bytes accessed | tf_op | source)
XLA Modules:
  0.0 54.5 jit_solution(7074966109833112857)
XLA Ops:
  0.0 52.9 %shard_map.91 = bf16[128,640]{1,0:T(8,128)(2,1)} custom-call(s32[1,1,16]{2,1,0:T(1,128)} %own_table.1, s32[1,1,16]{2,1,0:T(1,128)} %own_table.1, bf16[16,192,128]{2,1,0:T(8,128)(2,1)} %bitcast.10, bf16[192,1024]{1,0:T(8,128)(2,1)} %bitcast.11, bf16[16,64,128]{2,1,0:T(8,128)(2,1)} %bitcast.12, bf16[64,192]{1,0:T(8,128)(2,1)} %bitcast.14, ...), custom_call_target="tpu_custom_call" | custom-call | tf_op jit(solution)/shard_map/pallas_call | solution.py:454
  52.9 1.6 %copy.11 = bf16[128,640]{1,0:T(8,128)(2,1)} copy(bf16[128,640]{1,0:T(8,128)(2,1)} %shard_map.91) | data formatting | bytes 327680

commit v4 on v3

--- a/solution.py
+++ b/solution.py
@@ -299,7 +299,7 @@
             top_ref[:, here] = new
             return carry
 
-        lax.fori_loop(0, heads * TILE // span, chunk, 0, unroll=4)
+        lax.fori_loop(0, heads * TILE // span, chunk, 0, unroll=8)
 
     values_wide[128:, :] = jnp.ones_like(values_wide[128:, :])
 

time: 54.7 us -> 54.4 us (level)
  no operation moved by 1% of the time
where the time goes in v4:
time: 54.4 us; the launch traced here: 54.2 us
  Pallas kernels  52.6 us (97%)
  local copies, waits for them, and re-layouts  1.6 us (3%)
    pallas_call x1, Pallas kernels, shards(): pl.pallas_call(functools.partial(kernel, n, groups, cap, width ** (-0.5)...  52.6 us
    unnamed x1, local copies, waits for them, and re-layouts  1.6 us

profile of v4, /device:TPU:8, one launch (start us, length us, event | category | flops | bytes accessed | tf_op | source)
XLA Modules:
  0.0 54.2 jit_solution(9984321401418810850)
XLA Ops:
  0.0 52.6 %shard_map.91 = bf16[128,640]{1,0:T(8,128)(2,1)} custom-call(s32[1,1,16]{2,1,0:T(1,128)} %own_table.1, s32[1,1,16]{2,1,0:T(1,128)} %own_table.1, bf16[16,192,128]{2,1,0:T(8,128)(2,1)} %bitcast.10, bf16[192,1024]{1,0:T(8,128)(2,1)} %bitcast.11, bf16[16,64,128]{2,1,0:T(8,128)(2,1)} %bitcast.12, bf16[64,192]{1,0:T(8,128)(2,1)} %bitcast.14, ...), custom_call_target="tpu_custom_call" | custom-call | tf_op jit(solution)/shard_map/pallas_call | solution.py:454
  52.6 1.6 %copy.11 = bf16[128,640]{1,0:T(8,128)(2,1)} copy(bf16[128,640]{1,0:T(8,128)(2,1)} %shard_map.91) | data formatting | bytes 327680
